TPU v7x, 512 devices: a whole 4x8x8 slice. The times are simulated.
512 devices in a mesh: dp: 64 (over x, y, z_hi), head: 8 (over z_lo, core).
Axes of the slice: x: 4, y: 8, z: 8 (z_hi: 2, z_lo: 4; z = z_hi * 4 + z_lo), core: 2. Of those that a mesh axis runs over, the one named last changes fastest.
Arguments:
- tokens: bfloat16 [16384, 8192], P('dp', 'head'), may hold values from -6 to 6
- key_weight: bfloat16 [8192, 1024], P('dp', 'head'), may hold values from -0.0625 to 0.0625
- queries: bfloat16 [16384, 8192], P('dp', 'head'), may hold values from -51 to 51
- values: bfloat16 [16384, 1024], P('dp', 'head'), may hold values from -6 to 6
- out_grad: bfloat16 [16384, 8192], P('dp', 'head'), may hold values from -6 to 6
Outputs:
- query_grad: bfloat16 [16384, 8192], P('dp', 'head')
- value_grad: bfloat16 [16384, 1024], P('dp', 'head')
- weight_grad: float32 [8192, 1024], P('dp', 'head')
All inputs are finite; a program needn't handle non-finite values.
Results may differ from a plain program's by a relative error of at most 0.022.
The roundings to bfloat16 on the way count: a program that leaves them out, or rounds other values in their place, can miss the bound.
Values may be sent and summed in bfloat16 or wider, within the bound.
No kernel may reach another device: no remote copies, remote signals or barrier semaphores. Data moves between devices by JAX's collectives and lax.ppermute only.
A program may use at most 64 MiB of HBM per device.

v0:
```python
import jax
import jax.numpy as jnp
from jax import lax
from jax.sharding import PartitionSpec as P


def on_device(tokens, key_weight, queries, values, out_grad):
    width = values.shape[1]
    length = tokens.shape[0]
    group = queries.shape[1] // width
    scale = width ** (-0.5)
    gathered = lax.all_gather(tokens, "head", axis=1, tiled=True)
    columns = gathered
    keys = jnp.dot(
        columns,
        lax.all_gather(key_weight, "dp", axis=0, tiled=True),
        preferred_element_type=jnp.float32,
    ).astype(jnp.bfloat16)
    query_heads = queries.reshape(length, group, width)
    grad_heads = out_grad.reshape(length, group, width)
    scores = (
        jnp.einsum("qgd,kd->gqk", query_heads, keys, preferred_element_type=jnp.float32) * scale
    )
    rows = lax.broadcasted_iota(jnp.int32, (length, length), 0)
    cols = lax.broadcasted_iota(jnp.int32, (length, length), 1)
    keep = rows >= cols
    scores = jnp.where(keep, scores, jnp.float32(-1e30))
    top = jnp.max(scores, axis=-1, keepdims=True)
    expo = jnp.where(keep, jnp.exp(scores - top), jnp.float32(0.0))
    probs = expo / jnp.sum(expo, axis=-1, keepdims=True)
    weights = probs.astype(jnp.bfloat16)
    attended = jnp.einsum(
        "gqk,kd->qgd", weights, values, preferred_element_type=jnp.float32
    ).astype(jnp.bfloat16)
    dprobs = jnp.einsum("qgd,kd->gqk", grad_heads, values, preferred_element_type=jnp.float32)
    delta = jnp.transpose(
        jnp.sum(grad_heads.astype(jnp.float32) * attended.astype(jnp.float32), axis=-1), (1, 0)
    )
    dscores = (probs * (dprobs - delta[..., None])).astype(jnp.bfloat16)
    query_grad = (
        jnp.einsum("gqk,kd->qgd", dscores, keys, preferred_element_type=jnp.float32) * scale
    ).astype(jnp.bfloat16)
    key_grad = (
        jnp.einsum("gqk,qgd->kd", dscores, query_heads, preferred_element_type=jnp.float32) * scale
    ).astype(jnp.bfloat16)
    value_grad = jnp.einsum(
        "gqk,qgd->kd", weights, grad_heads, preferred_element_type=jnp.float32
    ).astype(jnp.bfloat16)
    columns = gathered
    weight_grad = lax.psum_scatter(
        lax.dot_general(
            columns, key_grad, (((0,), (0,)), ((), ())), preferred_element_type=jnp.float32
        ),
        "dp",
        scatter_dimension=0,
        tiled=True,
    )
    return (query_grad.reshape(length, group * width), value_grad, weight_grad)


def solution(mesh):
    placed = (P("dp", "head"), P("dp", "head"), P("dp", "head"), P("dp", "head"), P("dp", "head"))
    return jax.shard_map(
        on_device,
        mesh=mesh,
        in_specs=placed,
        out_specs=(P("dp", "head"), P("dp", "head"), P("dp", "head")),
        check_vma=False,
    )
```

profile of v0, /device:TPU:64, one launch (start us, length us, event | category | flops | bytes accessed | tf_op | source)
XLA Modules:
  0.0 685.2 jit_solution(2538484777238833299)
XLA Ops:
  7.2 0.0 copy-start
  7.2 0.0 all-gather.5.cloned.1.call-start
  7.2 0.7 all-gather.5.cloned.1.call-update
  7.9 0.0 all-gather.3.cloned.1.call-start
  8.0 0.7 all-gather.3.cloned.1.call-update
  8.7 0.0 reduce-scatter.2.cloned.1.call-start
  8.7 1.2 copy.9
  10.0 144.5 %all-gather.5.cloned.1.call-done = bf16[8192,128]{1,0:T(8,128)(2,1)} async-done(((bf16[128,128]{1,0:T(8,128)(2,1)}), bf16[8192,128]{1,0:T(8,128)(2,1)}) %all-gather.5.cloned.1.call-update) | async-done | bytes 2097168 | tf_op jit(solution)/shard_map/all_gather | solution.py:16
  154.5 48.9 %all-gather.3.cloned.1.call-done = bf16[256,8192]{1,0:T(8,128)(2,1)} async-done(((bf16[256,1024]{1,0:T(8,128)(2,1)}), bf16[256,8192]{1,0:T(8,128)(2,1)}) %all-gather.3.cloned.1.call-update) | async-done | bytes 4194320 | tf_op jit(solution)/shard_map/all_gather | solution.py:12
  203.5 4.1 fusion.12
  207.6 0.0 copy-done
  207.6 2.3 fusion.36
  209.8 0.0 copy-start.2
  209.8 0.0 copy-start.1
  209.8 1.9 fusion.16
  211.8 0.0 copy-done.2
  211.8 0.4 fusion.8
  212.2 0.0 copy-done.1
  212.2 0.4 fusion.2
  212.6 5.3 convolution_bitcast_fusion
  217.9 0.0 reduce-scatter.2.cloned.1.call-update
  217.9 1.1 fusion.7
  219.0 2.0 copy.16
  221.1 1.1 fusion.10
  222.1 454.9 %reduce-scatter.2.cloned.1.call-done = f32[128,128]{0,1:T(8,128)} async-done(((f32[8192,128]{0,1:T(8,128)}), f32[128,128]{0,1:T(8,128)}) %reduce-scatter.2.cloned.1.call-update) | async-done | bytes 65552 | tf_op jit(solution)/shard_map/reduce_scatter | solution.py:50
  677.1 1.6 copy.17
  (1 shorter events, 0.0 us)
Async XLA Ops:
  7.2 200.4 %copy-start = (bf16[256,1024]{1,0:T(8,128)(2,1)S(1)}, bf16[256,1024]{1,0:T(8,128)(2,1)}, u32[]{:S(2)}) copy-start(bf16[256,1024]{1,0:T(8,128)(2,1)} %param.7) | copy-start | bytes 1572868
  7.2 147.4 %all-gather.5.cloned.1.call-start = ((), (), s32[]{:S(2)}) async-start(), calls=%async_computation.2 | async-start | bytes 2129920 | tf_op jit(solution)/shard_map/all_gather | solution.py:16
  7.9 195.5 %all-gather.3.cloned.1.call-start = ((), (), s32[]{:S(2)}) async-start(), calls=%async_computation.1 | async-start | bytes 4718592 | tf_op jit(solution)/shard_map/all_gather | solution.py:12
  8.7 668.4 %reduce-scatter.2.cloned.1.call-start = ((), (), s32[]{:S(2)}) async-start(), calls=%async_computation.3 | async-start | bytes 4259840 | tf_op jit(solution)/shard_map/reduce_scatter | solution.py:50
  209.8 1.9 copy-start.2
  209.8 2.3 copy-start.1
Sparse Core Ops, SparseCore 0:
  12.5 141.9 all-gather.4
  156.6 46.7 all-gather.2
  218.1 458.9 reduce-scatter.1
where the time goes:
time: 685 us
  waiting for transfers between devices  650 us (95%)
  matrix products  14.7 us (2%)
  between operations  13.8 us (2%)
    reduce_scatter x1, waiting for transfers between devices, on_device(): lax.psum_scatter(lax.dot_general(columns, key_grad, (((0,), (0,)), ((), (...  455 us
    all_gather x1, waiting for transfers between devices, on_device(): lax.all_gather(key_weight, 'dp', axis=0, tiled=True)  145 us
    all_gather x1, waiting for transfers between devices, on_device(): gathered = lax.all_gather(tokens, 'head', axis=1, tiled=True)  48.9 us
  transfers between devices with their start and end apart: 3, of which 3 were waited for; matrix products, arithmetic and copies ran while one was open for 1% of the time, Pallas kernels for 0%

commit v1 on v0

--- a/solution.py
+++ b/solution.py
@@ -11,10 +11,14 @@
     scale = width ** (-0.5)
     gathered = lax.all_gather(tokens, "head", axis=1, tiled=True)
     columns = gathered
+
+    def begin_islands_for(array_in, dim_no):
+        side_arr = jnp.stack([array_in for _ in range(lax.axis_size("dp"))], axis=0)
+        high = lax.all_to_all(side_arr, "dp", 0, 0)
+        return jnp.concatenate(high, dim_no)
+
     keys = jnp.dot(
-        columns,
-        lax.all_gather(key_weight, "dp", axis=0, tiled=True),
-        preferred_element_type=jnp.float32,
+        columns, begin_islands_for(key_weight, 0), preferred_element_type=jnp.float32
     ).astype(jnp.bfloat16)
     query_heads = queries.reshape(length, group, width)
     grad_heads = out_grad.reshape(length, group, width)

time: 685 us -> 592 us (0.86)
  waiting for transfers between devices: 650 us -> 536 us
  starting transfers between devices: 0.11 us -> 18.2 us
    all_gather x1 -> x0, waiting for transfers between devices: 145 us -> none  [on_device(): lax.all_gather(key_weight, 'dp', axis=0, tiled=True)]
    all_to_all x0 -> x1, waiting for transfers between devices: none -> 55.2 us  [begin_islands_for(): high = lax.all_to_all(side_arr, 'dp', 0, 0)]
    all_gather x1, waiting for transfers between devices: 48.9 us -> 27.5 us  [on_device(): gathered = lax.all_gather(tokens, 'head', axis=1, tiled=True)]
    all_to_all x0 -> x1, starting transfers between devices: none -> 18.1 us  [begin_islands_for(): high = lax.all_to_all(side_arr, 'dp', 0, 0)]
where the time goes in v1:
time: 592 us
  waiting for transfers between devices  536 us (91%)
  starting transfers between devices  18.2 us (3%)
  between operations  14.1 us (2%)
  matrix products  14 us (2%)
  local copies, waits for them, and re-layouts  7.46 us (1%)
    reduce_scatter x1, waiting for transfers between devices, on_device(): lax.psum_scatter(lax.dot_general(columns, key_grad, (((0,), (0,)), ((), (...  453 us
    all_to_all x1, waiting for transfers between devices, begin_islands_for(): high = lax.all_to_all(side_arr, 'dp', 0, 0)  55.2 us
    all_gather x1, waiting for transfers between devices, on_device(): gathered = lax.all_gather(tokens, 'head', axis=1, tiled=True)  27.5 us
    all_to_all x1, starting transfers between devices, begin_islands_for(): high = lax.all_to_all(side_arr, 'dp', 0, 0)  18.1 us
  transfers between devices with their start and end apart: 3, of which 3 were waited for; matrix products, arithmetic and copies ran while one was open for 1% of the time, Pallas kernels for 0%

profile of v1, /device:TPU:64, one launch (start us, length us, event | category | flops | bytes accessed | tf_op | source)
XLA Modules:
  0.0 592.0 jit_solution(14355670110173507590)
XLA Ops:
  7.2 0.0 copy-start
  7.2 0.0 all-gather.2.cloned.1.call-start
  7.2 0.7 all-gather.2.cloned.1.call-update
  7.9 2.6 stack.2
  10.5 18.1 %all-to-all-start = ((bf16[64,128,128]{2,1,0:T(8,128)(2,1)}), bf16[64,128,128]{2,1,0:T(8,128)(2,1)S(1)}, u32[]{:S(2)}, u32[]{:S(2)}) async-start(bf16[64,128,128]{2,1,0:T(8,128)(2,1)} %stack.2), calls=%async_computation | async-start | bytes 4194304 | tf_op jit(solution)/shard_map/all_to_all | solution.py:17
  28.6 0.0 reduce-scatter.2.cloned.1.call-start
  28.7 1.2 copy.9
  30.0 55.2 %all-to-all-done = bf16[64,128,128]{2,1,0:T(8,128)(2,1)S(1)} async-done(((bf16[64,128,128]{2,1,0:T(8,128)(2,1)}), bf16[64,128,128]{2,1,0:T(8,128)(2,1)S(1)}, u32[]{:S(2)}, u32[]{:S(2)}) %all-to-all-start) | async-done | bytes 2097184 | tf_op jit(solution)/shard_map/all_to_all | solution.py:17
  85.1 27.5 %all-gather.2.cloned.1.call-done = bf16[256,8192]{1,0:T(8,128)(2,1)} async-done(((bf16[256,1024]{1,0:T(8,128)(2,1)}), bf16[256,8192]{1,0:T(8,128)(2,1)}) %all-gather.2.cloned.1.call-update) | async-done | bytes 4194320 | tf_op jit(solution)/shard_map/all_gather | solution.py:12
  112.6 3.4 fusion.12
  116.1 0.0 copy-done
  116.1 2.3 fusion.36
  118.4 0.0 copy-start.2
  118.4 0.0 copy-start.1
  118.4 1.9 fusion.16
  120.3 0.0 copy-done.2
  120.3 0.4 fusion.8
  120.7 0.0 copy-done.1
  120.7 0.4 fusion.2
  121.1 5.3 convolution_bitcast_fusion
  126.4 0.0 reduce-scatter.2.cloned.1.call-update
  126.5 1.1 fusion.7
  127.6 2.0 copy.16
  129.6 1.1 fusion.10
  130.7 452.9 %reduce-scatter.2.cloned.1.call-done = f32[128,128]{0,1:T(8,128)} async-done(((f32[8192,128]{0,1:T(8,128)}), f32[128,128]{0,1:T(8,128)}) %reduce-scatter.2.cloned.1.call-update) | async-done | bytes 65552 | tf_op jit(solution)/shard_map/reduce_scatter | solution.py:54
  583.6 1.6 copy.17
  (1 shorter events, 0.0 us)
Async XLA Ops:
  7.2 108.9 %copy-start = (bf16[256,1024]{1,0:T(8,128)(2,1)S(1)}, bf16[256,1024]{1,0:T(8,128)(2,1)}, u32[]{:S(2)}) copy-start(bf16[256,1024]{1,0:T(8,128)(2,1)} %param.7) | copy-start | bytes 1572868
  7.2 105.5 %all-gather.2.cloned.1.call-start = ((), (), s32[]{:S(2)}) async-start(), calls=%async_computation.2 | async-start | bytes 4718592 | tf_op jit(solution)/shard_map/all_gather | solution.py:12
  10.5 74.6 %all-to-all-start = ((bf16[64,128,128]{2,1,0:T(8,128)(2,1)}), bf16[64,128,128]{2,1,0:T(8,128)(2,1)S(1)}, u32[]{:S(2)}, u32[]{:S(2)}) async-start(bf16[64,128,128]{2,1,0:T(8,128)(2,1)} %stack.2), calls=%async_computation | async-start | bytes 4194304 | tf_op jit(solution)/shard_map/all_to_all | solution.py:17
  28.6 554.9 %reduce-scatter.2.cloned.1.call-start = ((), (), s32[]{:S(2)}) async-start(), calls=%async_computation.3 | async-start | bytes 4259840 | tf_op jit(solution)/shard_map/reduce_scatter | solution.py:54
  118.4 1.9 copy-start.2
  118.4 2.3 copy-start.1
Sparse Core Ops, SparseCore 0:
  10.1 102.5 all-gather.1
  126.6 456.9 reduce-scatter.1
